TPU v7x, 128 devices: a whole 4x4x4 slice. The times are simulated.
128 devices in a mesh: blk: 16 (over x, z), beam: 8 (over y, core).
Axes of the slice: x: 4, y: 4, z: 4, core: 2. Of those that a mesh axis runs over, the one named last changes fastest.
Arguments:
- embeds: bfloat16 [4, 128, 2048], P(None, 'beam'), may hold values from -6 to 6
- attn_gain: float32 [2048], replicated, may hold values from 0.25 to 1.75
- w_query: bfloat16 [2048, 3072], P(None, 'blk'), may hold values from -0.125 to 0.125
- w_latent: bfloat16 [2048, 576], replicated, may hold values from -0.125 to 0.125
- latent_gain: float32 [512], replicated, may hold values from 0.3 to 3
- w_key_up: bfloat16 [16, 128, 512], P('blk'), may hold values from -0.5 to 0.5
- w_value_up: bfloat16 [16, 512, 128], P('blk'), may hold values from -0.25 to 0.25
- w_out: bfloat16 [2048, 2048], P('blk'), may hold values from -0.125 to 0.125
- ffn_gain: float32 [2048], replicated, may hold values from 0.25 to 1.75
- w_shared_gate: bfloat16 [2048, 2816], P(None, 'blk'), may hold values from -0.125 to 0.125
- w_shared_up: bfloat16 [2048, 2816], P(None, 'blk'), may hold values from -0.125 to 0.125
- w_shared_down: bfloat16 [2816, 2048], P('blk'), may hold values from -0.109375 to 0.109375
- w_expert_gate: bfloat16 [32, 2048, 2816], P('blk', None, 'beam'), may hold values from -0.125 to 0.125
- w_expert_up: bfloat16 [32, 2048, 2816], P('blk', None, 'beam'), may hold values from -0.125 to 0.125
- w_expert_down: bfloat16 [32, 2816, 2048], P('blk', 'beam'), may hold values from -0.15625 to 0.15625
- cache_pool: bfloat16 [16, 96, 128, 576], P('beam', 'blk'), may hold values from -1600 to 1600
- block_tables: int32 [16, 8, 64], P('beam'), may hold values from 0 to 95, as said below
- block_counts: int32 [16], P('beam'), may hold values from 4 to 64
- parents: int32 [4, 16, 8], P(None, 'beam'), may hold values from 0 to 7
- expert_ids: int32 [4, 128, 6], replicated, may hold values from 0 to 63, all different within a row; in each aligned block of 128 rows (0 to 127, 128 to 255, ..., all dimensions but the last counted through in order) at most 24 rows name the same one
- expert_weights: float32 [4, 128, 6], replicated, may hold values from 0.1 to 0.6
Outputs:
- layer_out: float32 [4, 128, 2048], P(None, ('blk', 'beam'))
Inputs may be any that keep to these rules, and one draw needn't show every extreme that they name: `block_tables`: for each group g, entries j below block_counts[g] of one beam name different physical blocks; entries at or beyond block_counts[g] are never read. `expert_ids`: the experts of one row differ; within one step all rows together name one expert at most 24 times.
All inputs are finite; a program needn't handle non-finite values.
Results may differ from a plain program's by a relative error of at most 0.034.
Values may be sent and summed in bfloat16 or wider, within the bound.
No kernel may reach another device: no remote copies, remote signals or barrier semaphores. Data moves between devices by JAX's collectives and lax.ppermute only.
A program may use at most 128 MiB of HBM per device.

v0:
```python
import jax
import jax.numpy as jnp
from jax import lax
from jax.sharding import PartitionSpec as P

EXPERTS = 64
FFE = 1408
THETA = 50000.0
EPS = 1e-06
NEG = -1e30


def combined_all(shard, axis, combine):
    everything = jax.tree.map(lambda part: lax.all_gather(part, axis), shard)
    initial = jax.tree.map(lambda part: part[0], everything)

    def step(k, so_far):
        return combine(so_far, jax.tree.map(lambda part: part[k], everything))

    return lax.fori_loop(1, lax.axis_size(axis), step, initial)


def rms_scale(values, gain):
    mean_sq = jnp.mean(values * values, axis=-1, keepdims=True)
    return values * lax.rsqrt(mean_sq + EPS) * gain


def rotate(values, position):
    half_dim = values.shape[-1] // 2
    frequency = THETA ** (-jnp.arange(half_dim, dtype=jnp.float32) * 2.0 / values.shape[-1])
    angles = position[..., None] * frequency
    cosine = jnp.cos(angles)
    sine_part = jnp.sin(angles)
    lower_half = values[..., :half_dim]
    upper_half = values[..., half_dim:]
    return jnp.concatenate(
        [
            lower_half * cosine - upper_half * sine_part,
            lower_half * sine_part + upper_half * cosine,
        ],
        axis=-1,
    )


def combine(earlier, later):
    top_first, sum_first, lat_first = earlier
    top_second, sum_second, lat_second = later
    top_score = jnp.maximum(top_first, top_second)
    scale_first = jnp.exp(top_first - top_score)
    scale_second = jnp.exp(top_second - top_score)
    return (
        top_score,
        sum_first * scale_first + sum_second * scale_second,
        lat_first * scale_first[..., None] + lat_second * scale_second[..., None],
    )


def partial_attend(scores, key_mask, values, form):
    masked = jnp.where(key_mask, scores, NEG)
    top_score = jnp.max(masked, axis=-1)
    weights = jnp.where(key_mask, jnp.exp(masked - top_score[..., None]), 0.0)
    weight_sum = jnp.sum(weights, axis=-1)
    latent_sum = jnp.einsum(
        form, weights.astype(jnp.bfloat16), values, preferred_element_type=jnp.float32
    )
    return (top_score, weight_sum, latent_sum)


def per_device(
    embeds,
    attn_gain,
    w_query,
    w_latent,
    latent_gain,
    w_key_up,
    w_value_up,
    w_out,
    ffn_gain,
    w_shared_gate,
    w_shared_up,
    w_shared_down,
    w_expert_gate,
    w_expert_up,
    w_expert_down,
    cache_pool,
    block_tables,
    block_counts,
    parents,
    expert_ids,
    expert_weights,
):
    step_count, row_dev, model_width = embeds.shape
    group_count, beam_count, max_blocks = block_tables.shape
    heads_dev, head_in, latent = w_key_up.shape
    entry_width = cache_pool.shape[3]
    pool_dev = cache_pool.shape[1]
    block_len = cache_pool.shape[2]
    value_dim = w_value_up.shape[2]
    pair_dev = w_expert_gate.shape[0]
    unit_dev = w_expert_gate.shape[2]
    topk_count = expert_ids.shape[2]
    blk_index = lax.axis_index("blk")
    beam_index = lax.axis_index("beam")
    total_rows = row_dev * lax.axis_size("beam")
    capacity = 2 * total_rows * topk_count // EXPERTS
    score_scale = (entry_width - latent + head_in) ** (-0.5)
    phys_ids = blk_index * pool_dev + jnp.arange(pool_dev, dtype=jnp.int32)
    cache_keys = cache_pool.reshape(group_count, pool_dev * block_len, entry_width)
    cache_values = cache_keys[:, :, :latent]
    recent = jnp.zeros((group_count, beam_count, step_count, entry_width), jnp.bfloat16)
    tables = block_tables
    base_pos = (block_counts * block_len).astype(jnp.float32)
    valid = jnp.arange(max_blocks, dtype=jnp.int32)[None, None, :] < block_counts[:, None, None]
    pair_half = beam_index * unit_dev // FFE
    local_experts = (blk_index * pair_dev + jnp.arange(pair_dev, dtype=jnp.int32)) * 2 + pair_half
    results = []
    for decode_step in range(step_count):
        parent = parents[decode_step]
        recent = jnp.take_along_axis(recent, parent[:, :, None, None], axis=1)
        tables = jnp.take_along_axis(tables, parent[:, :, None], axis=1)
        tokens = embeds[decode_step]
        normed = rms_scale(tokens.astype(jnp.float32), attn_gain).astype(jnp.bfloat16)
        queries = jnp.dot(normed, w_query, preferred_element_type=jnp.float32).astype(jnp.bfloat16)
        queries = queries.reshape(row_dev, heads_dev, w_query.shape[1] // heads_dev)
        position = jnp.repeat(base_pos + decode_step, beam_count)
        query_latent = jnp.einsum(
            "rhn,hnc->rhc", queries[:, :, :head_in], w_key_up, preferred_element_type=jnp.float32
        )
        query_rope = rotate(queries[:, :, head_in:].astype(jnp.float32), position[:, None])
        query_full = jnp.concatenate([query_latent, query_rope], axis=-1).astype(jnp.bfloat16)
        projected = jnp.dot(normed, w_latent, preferred_element_type=jnp.float32)
        new_entry = jnp.concatenate(
            [
                rms_scale(projected[:, :latent], latent_gain),
                rotate(projected[:, latent:], position),
            ],
            axis=-1,
        ).astype(jnp.bfloat16)
        recent = recent.at[:, :, decode_step].set(
            new_entry.reshape(group_count, beam_count, entry_width)
        )
        all_queries = lax.all_gather(query_full, "blk", axis=1, tiled=True)
        head_count = all_queries.shape[1]
        grouped = all_queries.reshape(group_count, beam_count * head_count, entry_width)
        scores = (
            jnp.einsum("gqe,gke->gqk", grouped, cache_keys, preferred_element_type=jnp.float32)
            * score_scale
        )
        block_used = (
            jnp.sum(
                ((tables[:, :, :, None] == phys_ids) & valid[..., None]).astype(jnp.int32), axis=2
            )
            > 0
        )
        key_mask = jnp.repeat(jnp.repeat(block_used, block_len, axis=2), head_count, axis=1)
        top_score, weight_sum, latent_sum = partial_attend(
            scores, key_mask, cache_values, "gqk,gkc->gqc"
        )
        top_score = top_score.reshape(row_dev, head_count)
        weight_sum = weight_sum.reshape(row_dev, head_count)
        latent_sum = latent_sum.reshape(row_dev, head_count, latent)
        merged = combined_all((top_score, weight_sum, latent_sum), "blk", combine)
        head_start = blk_index * heads_dev
        pooled = tuple(
            (lax.dynamic_slice_in_dim(member, head_start, heads_dev, 1) for member in merged)
        )
        recent_rows = recent.reshape(row_dev, step_count, entry_width)[:, : decode_step + 1]
        recent_scores = (
            jnp.einsum("rhe,rse->rhs", query_full, recent_rows, preferred_element_type=jnp.float32)
            * score_scale
        )
        recent_part = partial_attend(
            recent_scores,
            jnp.ones(recent_scores.shape, bool),
            recent_rows[:, :, :latent],
            "rhs,rsc->rhc",
        )
        top_score, weight_sum, latent_sum = combine(pooled, recent_part)
        attended = (latent_sum / weight_sum[..., None]).astype(jnp.bfloat16)
        head_out = jnp.einsum(
            "rhc,hcv->rhv", attended, w_value_up, preferred_element_type=jnp.float32
        ).astype(jnp.bfloat16)
        attn_part = jnp.dot(
            head_out.reshape(row_dev, heads_dev * value_dim),
            w_out,
            preferred_element_type=jnp.float32,
        )
        attn_total = lax.psum(attn_part, "blk")
        resid = tokens.astype(jnp.float32) + attn_total
        ffn_in = rms_scale(resid, ffn_gain).astype(jnp.bfloat16)
        all_rows = lax.all_gather(ffn_in, "beam", axis=0, tiled=True)
        matches = expert_ids[decode_step][:, :, None] == local_experts
        routed = jnp.any(matches, axis=1)
        row_weight = jnp.sum(
            jnp.where(matches, expert_weights[decode_step][:, :, None], 0.0), axis=1
        )
        slot_index = jnp.cumsum(routed.astype(jnp.int32), axis=0) - 1
        slot_index = jnp.where(routed, slot_index, capacity)
        expert_cols = jnp.broadcast_to(
            jnp.arange(pair_dev, dtype=jnp.int32)[None, :], (total_rows, pair_dev)
        )
        row_numbers = jnp.broadcast_to(
            jnp.arange(total_rows, dtype=jnp.int32)[:, None], (total_rows, pair_dev)
        )
        slot_rows = (
            jnp.full((pair_dev, capacity), total_rows, jnp.int32)
            .at[expert_cols, slot_index]
            .set(row_numbers, mode="drop")
        )
        weight_pad = jnp.concatenate([row_weight.T, jnp.zeros((pair_dev, 1), jnp.float32)], axis=1)
        slot_weight = jnp.take_along_axis(weight_pad, slot_rows, axis=1)
        picked = jnp.take(all_rows, slot_rows, axis=0, mode="fill", fill_value=0)
        gate_val = jnp.einsum(
            "ecd,edf->ecf", picked, w_expert_gate, preferred_element_type=jnp.float32
        )
        up_val = jnp.einsum("ecd,edf->ecf", picked, w_expert_up, preferred_element_type=jnp.float32)
        activation = (jax.nn.silu(gate_val) * up_val).astype(jnp.bfloat16)
        down_out = (
            jnp.einsum(
                "ecf,efd->ecd", activation, w_expert_down, preferred_element_type=jnp.float32
            )
            * slot_weight[..., None]
        )
        partial_term = (
            jnp.zeros((total_rows, model_width), jnp.float32)
            .at[slot_rows.reshape(-1)]
            .add(down_out.reshape(-1, model_width), mode="drop")
        )
        shared_act = (
            jax.nn.silu(jnp.dot(ffn_in, w_shared_gate, preferred_element_type=jnp.float32))
            * jnp.dot(ffn_in, w_shared_up, preferred_element_type=jnp.float32)
        ).astype(jnp.bfloat16)
        own_rows = jnp.dot(
            shared_act, w_shared_down, preferred_element_type=jnp.float32
        ) + jnp.where(blk_index == 0, resid, 0.0)
        row_start = beam_index * row_dev
        partial_term = lax.dynamic_update_slice_in_dim(
            partial_term,
            lax.dynamic_slice_in_dim(partial_term, row_start, row_dev, 0) + own_rows,
            row_start,
            0,
        )
        summed = lax.psum_scatter(partial_term, ("blk", "beam"), scatter_dimension=0, tiled=True)
        results.append(summed)
    return jnp.stack(results)


def solution(mesh):
    placed = (
        P(None, "beam", None),
        P(),
        P(None, "blk"),
        P(),
        P(),
        P("blk", None, None),
        P("blk", None, None),
        P("blk", None),
        P(),
        P(None, "blk"),
        P(None, "blk"),
        P("blk", None),
        P("blk", None, "beam"),
        P("blk", None, "beam"),
        P("blk", "beam", None),
        P("beam", "blk", None, None),
        P("beam", None, None),
        P("beam"),
        P(None, "beam", None),
        P(),
        P(),
    )
    return jax.shard_map(
        per_device,
        mesh=mesh,
        in_specs=placed,
        out_specs=P(None, ("blk", "beam"), None),
        check_vma=False,
    )
```

profile of v0, /device:TPU:1, one launch (start us, length us, event | category | flops | bytes accessed | tf_op | source)
XLA Modules:
  0.0 969.4 jit_solution(11336190134766764950)
XLA Ops:
  19.6 20.8 %all_gather.60 = bf16[16,16,576]{2,0,1:T(8,128)(2,1)S(1)} all-gather(bf16[16,1,576]{2,0,1:T(8,128)(2,1)S(1)} %pad_maximum_fusion.4), channel_id=1, replica_groups=mesh['blk'=16,'beam'=8] {'blk'}, dimensions={1}, use_global_device_ids=true | all-gather | bytes 313344 | tf_op jit(solution)/shard_map/all_gather | solution.py:142
  40.4 3.9 copy.230
  44.4 2.5 fusion.389
  55.1 18.1 %all_gather.65 = bf16[16,16,576]{2,0,1:T(8,128)(2,1)S(1)} all-gather(bf16[16,1,576]{2,0,1:T(8,128)(2,1)S(1)} %pad_maximum_fusion.5), channel_id=1, replica_groups=mesh['blk'=16,'beam'=8] {'blk'}, dimensions={1}, use_global_device_ids=true | all-gather | bytes 313344 | tf_op jit(solution)/shard_map/all_gather | solution.py:142
  77.3 19.4 %all_gather.70 = bf16[16,16,576]{2,0,1:T(8,128)(2,1)S(1)} all-gather(bf16[16,1,576]{2,0,1:T(8,128)(2,1)S(1)} %pad_maximum_fusion.6), channel_id=1, replica_groups=mesh['blk'=16,'beam'=8] {'blk'}, dimensions={1}, use_global_device_ids=true | all-gather | bytes 313344 | tf_op jit(solution)/shard_map/all_gather | solution.py:142
  96.9 2.4 fusion.391
  102.2 19.3 %all_gather.75 = bf16[16,16,576]{2,0,1:T(8,128)(2,1)S(1)} all-gather(bf16[16,1,576]{2,0,1:T(8,128)(2,1)S(1)} %pad_maximum_fusion.7), channel_id=1, replica_groups=mesh['blk'=16,'beam'=8] {'blk'}, dimensions={1}, use_global_device_ids=true | all-gather | bytes 313344 | tf_op jit(solution)/shard_map/all_gather | solution.py:142
  121.7 2.4 fusion.392
  130.3 11.5 %scatter_fusion.3 = s32[2,24]{1,0:T(2,128)S(1)} fusion(s32[2,24]{1,0:T(2,128)S(1)} %broadcast.828.clone, s32[256]{0:T(256)S(1)} %reshape.1849, s32[256]{0:T(256)S(1)} %reshape.1809), kind=kCustom, calls=%fused_computation.22 | custom fusion | bytes 5120 | tf_op jit(solution)/shard_map/scatter | solution.py:208
  143.6 2.6 fusion.298
  146.2 2.4 fusion.289
  158.6 11.5 %scatter_fusion.2 = s32[2,24]{1,0:T(2,128)S(1)} fusion(s32[2,24]{1,0:T(2,128)S(1)} %broadcast.828.clone.1, s32[256]{0:T(256)S(1)} %reshape.1835, s32[256]{0:T(256)S(1)} %reshape.1809), kind=kCustom, calls=%fused_computation.20 | custom fusion | bytes 5120 | tf_op jit(solution)/shard_map/scatter | solution.py:208
  175.3 11.5 %scatter_fusion.1 = s32[2,24]{1,0:T(2,128)S(1)} fusion(s32[2,24]{1,0:T(2,128)S(1)} %broadcast.828.clone.2, s32[256]{0:T(256)S(1)} %reshape.1821, s32[256]{0:T(256)S(1)} %reshape.1809), kind=kCustom, calls=%fused_computation.18 | custom fusion | bytes 5120 | tf_op jit(solution)/shard_map/scatter | solution.py:208
  192.1 11.5 %scatter_fusion = s32[2,24]{1,0:T(2,128)S(1)} fusion(s32[2,24]{1,0:T(2,128)S(1)} %broadcast.828.clone.3, s32[256]{0:T(256)S(1)} %reshape.1807, s32[256]{0:T(256)S(1)} %reshape.1809), kind=kCustom, calls=%fused_computation.16 | custom fusion | bytes 5120 | tf_op jit(solution)/shard_map/scatter | solution.py:208
  209.0 19.1 %all_gather.61 = f32[16,16,16]{2,1,0:T(8,128)S(1)} all-gather(f32[1,16,16]{2,1,0:T(8,128)S(1)} %all_gather_reshape.36), channel_id=1, replica_groups=mesh['blk'=16,'beam'=8] {'blk'}, dimensions={0}, use_global_device_ids=true | all-gather | bytes 17408 | tf_op jit(solution)/shard_map/all_gather | solution.py:14
  228.2 18.1 %all_gather.62 = f32[16,16,16]{2,1,0:T(8,128)S(1)} all-gather(f32[1,16,16]{2,1,0:T(8,128)S(1)} %all_gather_reshape.37), channel_id=1, replica_groups=mesh['blk'=16,'beam'=8] {'blk'}, dimensions={0}, use_global_device_ids=true | all-gather | bytes 17408 | tf_op jit(solution)/shard_map/all_gather | solution.py:14
  252.9 19.4 %all_gather.66 = f32[16,16,16]{2,1,0:T(8,128)S(1)} all-gather(f32[1,16,16]{2,1,0:T(8,128)S(1)} %all_gather_reshape.39), channel_id=1, replica_groups=mesh['blk'=16,'beam'=8] {'blk'}, dimensions={0}, use_global_device_ids=true | all-gather | bytes 17408 | tf_op jit(solution)/shard_map/all_gather | solution.py:14
  273.0 16.5 %all_gather.67 = f32[16,16,16]{2,1,0:T(8,128)S(1)} all-gather(f32[1,16,16]{2,1,0:T(8,128)S(1)} %all_gather_reshape.40), channel_id=1, replica_groups=mesh['blk'=16,'beam'=8] {'blk'}, dimensions={0}, use_global_device_ids=true | all-gather | bytes 17408 | tf_op jit(solution)/shard_map/all_gather | solution.py:14
  295.8 18.2 %all_gather.71 = f32[16,16,16]{2,1,0:T(8,128)S(1)} all-gather(f32[1,16,16]{2,1,0:T(8,128)S(1)} %all_gather_reshape.42), channel_id=1, replica_groups=mesh['blk'=16,'beam'=8] {'blk'}, dimensions={0}, use_global_device_ids=true | all-gather | bytes 17408 | tf_op jit(solution)/shard_map/all_gather | solution.py:14
  314.8 18.2 %all_gather.72 = f32[16,16,16]{2,1,0:T(8,128)S(1)} all-gather(f32[1,16,16]{2,1,0:T(8,128)S(1)} %all_gather_reshape.43), channel_id=1, replica_groups=mesh['blk'=16,'beam'=8] {'blk'}, dimensions={0}, use_global_device_ids=true | all-gather | bytes 17408 | tf_op jit(solution)/shard_map/all_gather | solution.py:14
  338.0 18.5 %all_gather.76 = f32[16,16,16]{2,1,0:T(8,128)S(1)} all-gather(f32[1,16,16]{2,1,0:T(8,128)} %all_gather_reshape.45), channel_id=1, replica_groups=mesh['blk'=16,'beam'=8] {'blk'}, dimensions={0}, use_global_device_ids=true | all-gather | bytes 17408 | tf_op jit(solution)/shard_map/all_gather | solution.py:14
  357.3 15.7 %all_gather.77 = f32[16,16,16]{2,1,0:T(8,128)S(1)} all-gather(f32[1,16,16]{2,1,0:T(8,128)S(1)} %all_gather_reshape.46), channel_id=1, replica_groups=mesh['blk'=16,'beam'=8] {'blk'}, dimensions={0}, use_global_device_ids=true | all-gather | bytes 17408 | tf_op jit(solution)/shard_map/all_gather | solution.py:14
  390.7 29.7 %while.80 = (s32[]{:T(128)}, f32[16,16]{1,0:T(8,128)S(1)}, f32[16,16]{1,0:T(8,128)S(1)}, f32[16,16,512]{2,1,0:T(8,128)S(1)}, f32[16,16,16]{2,1,0:T(8,128)}, /*in...) while((s32[]{:T(128)}, f32[16,16]{1,0:T(8,128)S(1)}, ...), condition=%wide.region_8.10_spmd, body=%wide.region_7.9_spmd.sunk | while | flops 394757 | bytes 1583255 | solution.py:20
  423.9 29.6 %while.81 = (s32[]{:T(128)}, f32[16,16]{1,0:T(8,128)S(1)}, f32[16,16]{1,0:T(8,128)S(1)}, f32[16,16,512]{2,1,0:T(8,128)S(1)}, f32[16,16,16]{2,1,0:T(8,128)}, /*in...) while((s32[]{:T(128)}, f32[16,16]{1,0:T(8,128)S(1)}, ...), condition=%wide.region_23.28_spmd, body=%wide.region_22.27_spmd.sunk | while | flops 394757 | bytes 1583255 | solution.py:20
  457.2 29.6 %while.82 = (s32[]{:T(128)}, f32[16,16]{1,0:T(8,128)S(1)}, f32[16,16]{1,0:T(8,128)S(1)}, f32[16,16,512]{2,1,0:T(8,128)S(1)}, f32[16,16,16]{2,1,0:T(8,128)}, /*in...) while((s32[]{:T(128)}, f32[16,16]{1,0:T(8,128)S(1)}, ...), condition=%wide.region_40.45_spmd, body=%wide.region_39.44_spmd.sunk | while | flops 394757 | bytes 1583255 | solution.py:20
  490.4 38.8 %while.83 = (s32[]{:T(128)}, f32[16,16]{1,0:T(8,128)S(1)}, f32[16,16]{1,0:T(8,128)}, f32[16,16,512]{2,1,0:T(8,128)S(1)}, f32[16,16,16]{2,1,0:T(8,128)}, /*index=...) while((s32[]{:T(128)}, f32[16,16]{1,0:T(8,128)S(1)}, ...), condition=%wide.region_57.62_spmd, body=%wide.region_56.61_spmd.sunk | while | flops 394757 | bytes 1583255 | solution.py:20
  544.6 134.9 %all-reduce.15.cloned.1.call-done = (f32[16,2048]{1,0:T(8,128)}, f32[16,2048]{1,0:T(8,128)}, f32[16,2048]{1,0:T(8,128)}, f32[16,2048]{1,0:T(8,128)}) async-done(((f32[16,2048]{1,0:T(8,128)}, f32[16,2048]{1,0:T(8,128)}, f32[16,2048]{1,0:T(8,128)}, f32[16,2048]{1,0:T(8,128)}), (f32[16,2048]{1,0:T(8,128)}, f32[16,2048]{1,0:T(8,128)}, f32[16,2048]{1,0:T(8,128)}, ...) | async-done | bytes 524304 | tf_op jit(solution)/shard_map/psum | solution.py:188
  682.2 16.4 %all_gather.79 = bf16[128,2048]{1,0:T(8,128)(2,1)} all-gather(bf16[16,2048]{1,0:T(8,128)(2,1)S(1)} %get-tuple-element.895), channel_id=1, replica_groups=mesh['blk'=16,'beam'=8] {'beam'}, dimensions={0}, use_global_device_ids=true | all-gather | bytes 589824 | tf_op jit(solution)/shard_map/all_gather | solution.py:191
  700.7 14.3 %all_gather.74 = bf16[128,2048]{1,0:T(8,128)(2,1)} all-gather(bf16[16,2048]{1,0:T(8,128)(2,1)S(1)} %get-tuple-element.894), channel_id=1, replica_groups=mesh['blk'=16,'beam'=8] {'beam'}, dimensions={0}, use_global_device_ids=true | all-gather | bytes 589824 | tf_op jit(solution)/shard_map/all_gather | solution.py:191
  715.9 14.3 %all_gather.69 = bf16[128,2048]{1,0:T(8,128)(2,1)} all-gather(bf16[16,2048]{1,0:T(8,128)(2,1)S(1)} %get-tuple-element.893), channel_id=1, replica_groups=mesh['blk'=16,'beam'=8] {'beam'}, dimensions={0}, use_global_device_ids=true | all-gather | bytes 589824 | tf_op jit(solution)/shard_map/all_gather | solution.py:191
  731.1 14.2 %all_gather.64 = bf16[128,2048]{1,0:T(8,128)(2,1)} all-gather(bf16[16,2048]{1,0:T(8,128)(2,1)S(1)} %get-tuple-element.892), channel_id=1, replica_groups=mesh['blk'=16,'beam'=8] {'beam'}, dimensions={0}, use_global_device_ids=true | all-gather | bytes 589824 | tf_op jit(solution)/shard_map/all_gather | solution.py:191
  748.3 2.7 fusion.67
  751.1 3.9 convolution_multiply_fusion
  755.0 2.6 scatter_custom_fusion.7
  759.7 3.4 fusion.66
  763.1 3.9 convolution_multiply_fusion.1
  767.1 2.7 scatter_custom_fusion.5
  769.8 2.7 fusion.13
  772.5 2.7 fusion.15
  777.3 3.4 fusion.65
  780.7 3.9 convolution_multiply_fusion.2
  784.6 2.8 scatter_custom_fusion.3
  787.5 2.7 fusion.17
  792.2 3.4 fusion.64
  795.5 3.9 convolution_multiply_fusion.3
  799.5 2.6 scatter_custom_fusion.1
  802.1 2.7 fusion.19
  804.8 153.5 %all-reduce.13.cloned.1.call-done = (f32[128,2048]{1,0:T(8,128)}, f32[128,2048]{1,0:T(8,128)}, f32[128,2048]{1,0:T(8,128)}, f32[128,2048]{1,0:T(8,128)}) async-done(((f32[128,2048]{1,0:T(8,128)}, f32[128,2048]{1,0:T(8,128)}, f32[128,2048]{1,0:T(8,128)}, f32[128,2048]{1,0:T(8,128)}), (f32[128,2048]{1,0:T(8,128)}, f32[128,2048]{1,0:T(8,128)}, f32[128,2048]{1,0:T(8,128)}, ...) | async-done | bytes 4194320
  (600 shorter events, 271.2 us)
Async XLA Ops:
  6.5 744.5 %copy-start = (bf16[2,352,2048]{2,1,0:T(8,128)(2,1)S(1)}, bf16[2,352,2048]{2,1,0:T(8,128)(2,1)}, u32[]{:S(2)}) copy-start(bf16[2,352,2048]{2,1,0:T(8,128)(2,1)} %param.59) | copy-start | bytes 8650756
  6.5 383.1 %all-gather.5.cloned.1.call-start = ((), (), s32[]{:S(2)}) async-start(), calls=%async_computation | async-start | bytes 8912896 | tf_op jit(solution)/shard_map/all_gather | solution.py:14
  49.0 373.9 %all-gather.7.cloned.1.call-start = ((), (), s32[]{:S(2)}) async-start(), calls=%async_computation.1 | async-start | bytes 8912896 | tf_op jit(solution)/shard_map/all_gather | solution.py:14
  49.5 23.9 %copy-start.2 = (bf16[2,6,128,576]{3,2,1,0:T(8,128)(2,1)S(1)}, bf16[2,6,128,576]{3,2,1,0:T(8,128)(2,1)}, u32[]{:S(2)}) copy-start(bf16[2,6,128,576]{3,2,1,0:T(8,128)(2,1)} %copy.230) | copy-start | bytes 5308420
  54.4 22.3 %copy-start.53 = (bf16[16,1,32]{2,0,1:T(8,128)(2,1)}, bf16[16,1,32]{2,0,1:T(8,128)(2,1)S(1)}, u32[]{:S(2)}) copy-start(bf16[16,1,32]{2,0,1:T(8,128)(2,1)S(1)} %get-tuple-element.955) | copy-start | bytes 3076
  54.4 22.3 %copy-start.55 = (bf16[16,1,32]{2,0,1:T(8,128)(2,1)}, bf16[16,1,32]{2,0,1:T(8,128)(2,1)S(1)}, u32[]{:S(2)}) copy-start(bf16[16,1,32]{2,0,1:T(8,128)(2,1)S(1)} %get-tuple-element.956) | copy-start | bytes 3076
  54.4 47.2 %copy-start.49 = (bf16[16,1,32]{2,0,1:T(8,128)(2,1)}, bf16[16,1,32]{2,0,1:T(8,128)(2,1)S(1)}, u32[]{:S(2)}) copy-start(bf16[16,1,32]{2,0,1:T(8,128)(2,1)S(1)} %get-tuple-element.912) | copy-start | bytes 3076
  54.4 47.2 %copy-start.51 = (bf16[16,1,32]{2,0,1:T(8,128)(2,1)}, bf16[16,1,32]{2,0,1:T(8,128)(2,1)S(1)}, u32[]{:S(2)}) copy-start(bf16[16,1,32]{2,0,1:T(8,128)(2,1)S(1)} %get-tuple-element.913) | copy-start | bytes 3076
  76.5 379.6 %all-gather.9.cloned.1.call-start = ((), (), s32[]{:S(2)}) async-start(), calls=%async_computation.2 | async-start | bytes 8912896 | tf_op jit(solution)/shard_map/all_gather | solution.py:14
  76.7 23.5 %copy-start.3 = (bf16[2,6,128,576]{3,2,1,0:T(8,128)(2,1)S(1)}, bf16[2,6,128,576]{3,2,1,0:T(8,128)(2,1)}, u32[]{:S(2)}) copy-start(bf16[2,6,128,576]{3,2,1,0:T(8,128)(2,1)} %copy.230) | copy-start | bytes 5308420
  101.4 387.8 %all-gather.11.cloned.1.call-start = ((), (), s32[]{:S(2)}) async-start(), calls=%async_computation.3 | async-start | bytes 8912896 | tf_op jit(solution)/shard_map/all_gather | solution.py:14
  101.6 23.5 %copy-start.4 = (bf16[2,6,128,576]{3,2,1,0:T(8,128)(2,1)S(1)}, bf16[2,6,128,576]{3,2,1,0:T(8,128)(2,1)}, u32[]{:S(2)}) copy-start(bf16[2,6,128,576]{3,2,1,0:T(8,128)(2,1)} %copy.230) | copy-start | bytes 5308420
  126.3 553.2 %all-reduce.15.cloned.1.call-start = ((), (), s32[]{:S(2)}) async-start(), calls=%async_computation.5 | async-start | bytes 1048576 | tf_op jit(solution)/shard_map/psum | solution.py:188
  126.6 15.2 %copy-start.73 = (s32[2]{0:T(128)}, s32[2]{0:T(128)S(1)}, u32[]{:S(2)}) copy-start(s32[2]{0:T(128)S(1)} %multiply_add_fusion) | copy-start | bytes 28
  192.0 14.4 %copy-start.37 = (s32[128,6]{0,1:T(8,128)S(1)}, s32[128,6]{0,1:T(8,128)}, u32[]{:S(2)}) copy-start(s32[128,6]{0,1:T(8,128)} %copy-done.36) | copy-start | bytes 9220
  192.0 14.4 %copy-start.39 = (s32[128,6]{0,1:T(8,128)S(1)}, s32[128,6]{0,1:T(8,128)}, u32[]{:S(2)}) copy-start(s32[128,6]{0,1:T(8,128)} %copy-done.38) | copy-start | bytes 9220
  192.1 15.2 %copy-start.83 = (s32[2,24,1]{1,0,2:T(2,128)S(1)}, s32[2,24,1]{1,0,2:T(2,128)}, u32[]{:S(2)}) copy-start(s32[2,24,1]{1,0,2:T(2,128)} %bitcast_or_fusion) | copy-start | bytes 580
  192.1 36.0 %copy-start.66 = (f32[2,128]{1,0:T(2,128)S(1)}, f32[2,128]{1,0:T(2,128)}, u32[]{:S(2)}) copy-start(f32[2,128]{1,0:T(2,128)} %get-tuple-element.891) | copy-start | bytes 3076
  192.1 54.2 %copy-start.29 = (bf16[16,512]{1,0:T(8,128)(2,1)S(1)}, bf16[16,512]{1,0:T(8,128)(2,1)}, u32[]{:S(2)}) copy-start(bf16[16,512]{1,0:T(8,128)(2,1)} %copy-done.28) | copy-start | bytes 49156
  192.1 54.2 %copy-start.46 = (bf16[16,1,32]{2,0,1:T(8,128)(2,1)S(1)}, bf16[16,1,32]{2,0,1:T(8,128)(2,1)}, u32[]{:S(2)}) copy-start(bf16[16,1,32]{2,0,1:T(8,128)(2,1)} %copy-done.45) | copy-start | bytes 3076
  192.1 54.2 %copy-start.48 = (bf16[16,1,32]{2,0,1:T(8,128)(2,1)S(1)}, bf16[16,1,32]{2,0,1:T(8,128)(2,1)}, u32[]{:S(2)}) copy-start(bf16[16,1,32]{2,0,1:T(8,128)(2,1)} %copy-done.47) | copy-start | bytes 3076
  192.1 58.9 %copy-start.35 = (bf16[16,512]{1,0:T(8,128)(2,1)S(1)}, bf16[16,512]{1,0:T(8,128)(2,1)}, u32[]{:S(2)}) copy-start(bf16[16,512]{1,0:T(8,128)(2,1)} %copy-done.34) | copy-start | bytes 49156
  192.1 58.9 %copy-start.58 = (bf16[16,1,32]{2,0,1:T(8,128)(2,1)S(1)}, bf16[16,1,32]{2,0,1:T(8,128)(2,1)}, u32[]{:S(2)}) copy-start(bf16[16,1,32]{2,0,1:T(8,128)(2,1)} %copy-done.57) | copy-start | bytes 3076
  192.1 58.9 %copy-start.60 = (bf16[16,1,32]{2,0,1:T(8,128)(2,1)S(1)}, bf16[16,1,32]{2,0,1:T(8,128)(2,1)}, u32[]{:S(2)}) copy-start(bf16[16,1,32]{2,0,1:T(8,128)(2,1)} %copy-done.59) | copy-start | bytes 3076
  203.6 90.4 %copy-start.33 = (bf16[16,512]{1,0:T(8,128)(2,1)S(1)}, bf16[16,512]{1,0:T(8,128)(2,1)}, u32[]{:S(2)}) copy-start(bf16[16,512]{1,0:T(8,128)(2,1)} %copy-done.32) | copy-start | bytes 49156
  203.6 90.4 %copy-start.54 = (bf16[16,1,32]{2,0,1:T(8,128)(2,1)S(1)}, bf16[16,1,32]{2,0,1:T(8,128)(2,1)}, u32[]{:S(2)}) copy-start(bf16[16,1,32]{2,0,1:T(8,128)(2,1)} %copy-done.53) | copy-start | bytes 3076
  203.6 90.4 %copy-start.56 = (bf16[16,1,32]{2,0,1:T(8,128)(2,1)S(1)}, bf16[16,1,32]{2,0,1:T(8,128)(2,1)}, u32[]{:S(2)}) copy-start(bf16[16,1,32]{2,0,1:T(8,128)(2,1)} %copy-done.55) | copy-start | bytes 3076
  203.6 132.3 %copy-start.31 = (bf16[16,512]{1,0:T(8,128)(2,1)S(1)}, bf16[16,512]{1,0:T(8,128)(2,1)}, u32[]{:S(2)}) copy-start(bf16[16,512]{1,0:T(8,128)(2,1)} %copy-done.30) | copy-start | bytes 49156
  203.6 132.3 %copy-start.50 = (bf16[16,1,32]{2,0,1:T(8,128)(2,1)S(1)}, bf16[16,1,32]{2,0,1:T(8,128)(2,1)}, u32[]{:S(2)}) copy-start(bf16[16,1,32]{2,0,1:T(8,128)(2,1)} %copy-done.49) | copy-start | bytes 3076
  203.6 132.3 %copy-start.52 = (bf16[16,1,32]{2,0,1:T(8,128)(2,1)S(1)}, bf16[16,1,32]{2,0,1:T(8,128)(2,1)}, u32[]{:S(2)}) copy-start(bf16[16,1,32]{2,0,1:T(8,128)(2,1)} %copy-done.51) | copy-start | bytes 3076
  228.1 19.0 %copy-start.26 = (f32[16,16,16]{2,1,0:T(8,128)}, f32[16,16,16]{2,1,0:T(8,128)S(1)}, u32[]{:S(2)}) copy-start(f32[16,16,16]{2,1,0:T(8,128)S(1)} %all_gather.61) | copy-start | bytes 49156
  272.2 41.8 %copy-start.24 = (f32[16,16,16]{2,1,0:T(8,128)}, f32[16,16,16]{2,1,0:T(8,128)S(1)}, u32[]{:S(2)}) copy-start(f32[16,16,16]{2,1,0:T(8,128)S(1)} %all_gather.66) | copy-start | bytes 49156
  273.0 111.9 %copy-start.81 = (s32[2,24]{1,0:T(2,128)S(1)}, s32[2,24]{1,0:T(2,128)}, u32[]{:S(2)}) copy-start(s32[2,24]{1,0:T(2,128)} %compare_select_fusion.13) | copy-start | bytes 580
  273.0 113.7 %copy-start.67 = (f32[128,2]{0,1:T(2,128)S(1)}, f32[128,2]{0,1:T(2,128)}, u32[]{:S(2)}) copy-start(f32[128,2]{0,1:T(2,128)} %get-tuple-element.793) | copy-start | bytes 3076
  295.0 94.0 %copy-start.82 = (s32[2,24]{1,0:T(2,128)S(1)}, s32[2,24]{1,0:T(2,128)}, u32[]{:S(2)}) copy-start(s32[2,24]{1,0:T(2,128)} %compare_select_fusion.15) | copy-start | bytes 580
  314.1 42.5 %copy-start.22 = (f32[16,16,16]{2,1,0:T(8,128)}, f32[16,16,16]{2,1,0:T(8,128)S(1)}, u32[]{:S(2)}) copy-start(f32[16,16,16]{2,1,0:T(8,128)S(1)} %all_gather.71) | copy-start | bytes 49156
  333.0 56.6 %copy-start.23 = (f32[16,16,16]{2,1,0:T(8,128)}, f32[16,16,16]{2,1,0:T(8,128)S(1)}, u32[]{:S(2)}) copy-start(f32[16,16,16]{2,1,0:T(8,128)S(1)} %all_gather.72) | copy-start | bytes 49156
  356.5 20.4 %copy-start.20 = (f32[16,16,16]{2,1,0:T(8,128)}, f32[16,16,16]{2,1,0:T(8,128)S(1)}, u32[]{:S(2)}) copy-start(f32[16,16,16]{2,1,0:T(8,128)S(1)} %all_gather.76) | copy-start | bytes 49156
  373.0 16.6 %copy-start.21 = (f32[16,16,16]{2,1,0:T(8,128)}, f32[16,16,16]{2,1,0:T(8,128)S(1)}, u32[]{:S(2)}) copy-start(f32[16,16,16]{2,1,0:T(8,128)S(1)} %all_gather.77) | copy-start | bytes 49156
  490.3 43.5 %copy-start.10 = (bf16[1,512,128]{2,1,0:T(8,128)(2,1)S(1)}, bf16[1,512,128]{2,1,0:T(8,128)(2,1)}, u32[]{:S(2)}) copy-start(bf16[1,512,128]{2,1,0:T(8,128)(2,1)} %param.51) | copy-start | bytes 393220
  530.2 149.3 %copy-start.8 = (bf16[4,16,2048]{2,1,0:T(8,128)(2,1)S(1)}, bf16[4,16,2048]{2,1,0:T(8,128)(2,1)}, u32[]{:S(2)}) copy-start(bf16[4,16,2048]{2,1,0:T(8,128)(2,1)} %param.45) | copy-start | bytes 786436
  530.2 150.8 %copy-start.63 = (f32[2048]{0:T(1024)S(1)}, f32[2048]{0:T(1024)}, u32[]{:S(2)}) copy-start(f32[2048]{0:T(1024)} %param.53) | copy-start | bytes 24580
  542.2 416.1 %all-reduce.13.cloned.1.call-start = ((), (), s32[]{:S(2)}) async-start(), calls=%async_computation.4 | async-start | bytes 8388608
  679.5 35.4 %copy-start.6 = (bf16[2048,176]{0,1:T(8,128)(2,1)S(1)}, bf16[2048,176]{0,1:T(8,128)(2,1)}, u32[]{:S(2)}) copy-start(bf16[2048,176]{0,1:T(8,128)(2,1)} %param.54) | copy-start | bytes 2162692
  682.2 63.1 %copy-start.15 = (bf16[16,2048]{1,0:T(8,128)(2,1)}, bf16[16,2048]{1,0:T(8,128)(2,1)S(1)}, u32[]{:S(2)}) copy-start(bf16[16,2048]{1,0:T(8,128)(2,1)S(1)} %get-tuple-element.893) | copy-start | bytes 196612
  682.2 63.1 %copy-start.16 = (bf16[16,2048]{1,0:T(8,128)(2,1)}, bf16[16,2048]{1,0:T(8,128)(2,1)S(1)}, u32[]{:S(2)}) copy-start(bf16[16,2048]{1,0:T(8,128)(2,1)S(1)} %get-tuple-element.894) | copy-start | bytes 196612
  682.2 63.1 %copy-start.18 = (bf16[16,2048]{1,0:T(8,128)(2,1)}, bf16[16,2048]{1,0:T(8,128)(2,1)S(1)}, u32[]{:S(2)}) copy-start(bf16[16,2048]{1,0:T(8,128)(2,1)S(1)} %get-tuple-element.895) | copy-start | bytes 196612
  700.7 47.7 %copy-start.76 = (pred[2,24]{1,0:T(4,128)(4,1)S(1)}, pred[2,24]{1,0:T(4,128)(4,1)}, u32[]{:S(2)}) copy-start(pred[2,24]{1,0:T(4,128)(4,1)} %compare_and_fusion) | copy-start | bytes 148
  (44 other events, 214.4 us)
Sparse Core Ops, SparseCore 0:
  49.1 78.4 all-gather.4
  129.8 70.4 all-gather.6
  202.5 71.7 all-gather.8
  276.2 71.4 all-gather.10
  542.4 137.1 all-reduce.14
  804.9 153.3 all-reduce.12
where the time goes:
time: 984 us; the launch traced here: 969 us
  waiting for transfers between devices  288 us (29%)
  blocking collectives  281 us (29%)
  other arithmetic  187 us (19%)
  local copies, waits for them, and re-layouts  113 us (11%)
  matrix products  82.2 us (8%)
  between operations  15.3 us (2%)
    unnamed x7, waiting for transfers between devices  154 us
    all_gather x8, blocking collectives, combined_all(): everything = jax.tree.map(lambda part: lax.all_gather(part, axis), shard)  144 us
    psum x1, waiting for transfers between devices, per_device(): attn_total = lax.psum(attn_part, 'blk')  135 us
    all_gather x4, blocking collectives, per_device(): all_queries = lax.all_gather(query_full, 'blk', axis=1, tiled=True)  77.6 us
    add x60, other arithmetic, combine(): lat_first * scale_first[..., None] + lat_second * scale_second[..., None]  72.7 us
    all_gather x4, blocking collectives, per_device(): all_rows = lax.all_gather(ffn_in, 'beam', axis=0, tiled=True)  59.2 us
    add x60, other arithmetic, combine(): sum_first * scale_first + sum_second * scale_second  53.2 us
    scatter x4, local copies, waits for them, and re-layouts, per_device(): slot_rows = jnp.full((pair_dev, capacity), total_rows, jnp.int32).at[expe...  45.8 us
  transfers between devices with their start and end apart: 6, of which 2 were waited for; matrix products, arithmetic and copies ran while one was open for 24% of the time, Pallas kernels for 0%

commit v1 on v0

--- a/solution.py
+++ b/solution.py
@@ -185,7 +185,7 @@
             w_out,
             preferred_element_type=jnp.float32,
         )
-        attn_total = lax.psum(attn_part, "blk")
+        attn_total = lax.all_gather(attn_part, axis_name="blk").sum(axis=0)
         resid = tokens.astype(jnp.float32) + attn_total
         ffn_in = rms_scale(resid, ffn_gain).astype(jnp.bfloat16)
         all_rows = lax.all_gather(ffn_in, "beam", axis=0, tiled=True)

time: 984 us -> 943 us (0.958)
  waiting for transfers between devices: 288 us -> 221 us
  other arithmetic: 187 us -> 215 us
    psum x1 -> x0, waiting for transfers between devices: 135 us -> none  [per_device(): attn_total = lax.psum(attn_part, 'blk')]
    all_gather x0 -> x4, waiting for transfers between devices: none -> 67.4 us  [per_device(): attn_total = lax.all_gather(attn_part, axis_name='blk').sum(axis=0)]
    add x60, other arithmetic: 53.2 us -> 81.8 us  [combine(): sum_first * scale_first + sum_second * scale_second]
    unnamed x7 -> x10, waiting for transfers between devices: 154 us -> 154 us
  transfers between devices with their start and end apart: 6 -> 9, of which waited for: 2 -> 3; matrix products, arithmetic and copies ran while one was open for 24% -> 34% of each run, Pallas kernels for 0% -> 0%
where the time goes in v1:
time: 943 us; the launch traced here: 928 us
  blocking collectives  282 us (30%)
  waiting for transfers between devices  221 us (23%)
  other arithmetic  215 us (23%)
  local copies, waits for them, and re-layouts  110 us (12%)
  matrix products  82.7 us (9%)
  between operations  14.9 us (2%)
    unnamed x10, waiting for transfers between devices  154 us
    all_gather x8, blocking collectives, combined_all(): everything = jax.tree.map(lambda part: lax.all_gather(part, axis), shard)  146 us
    add x60, other arithmetic, combine(): sum_first * scale_first + sum_second * scale_second  81.8 us
    all_gather x4, blocking collectives, per_device(): all_queries = lax.all_gather(query_full, 'blk', axis=1, tiled=True)  77.2 us
    add x60, other arithmetic, combine(): lat_first * scale_first[..., None] + lat_second * scale_second[..., None]  72.4 us
    all_gather x4, waiting for transfers between devices, per_device(): attn_total = lax.all_gather(attn_part, axis_name='blk').sum(axis=0)  67.4 us
    all_gather x4, blocking collectives, per_device(): all_rows = lax.all_gather(ffn_in, 'beam', axis=0, tiled=True)  58.9 us
    scatter x4, local copies, waits for them, and re-layouts, per_device(): slot_rows = jnp.full((pair_dev, capacity), total_rows, jnp.int32).at[expe...  45.8 us
  transfers between devices with their start and end apart: 9, of which 3 were waited for; matrix products, arithmetic and copies ran while one was open for 34% of the time, Pallas kernels for 0%

profile of v1, /device:TPU:1, one launch (start us, length us, event | category | flops | bytes accessed | tf_op | source)
XLA Modules:
  0.0 928.1 jit_solution(6476480056673894762)
XLA Ops:
  19.0 20.8 %all_gather.84 = bf16[16,16,576]{2,0,1:T(8,128)(2,1)S(1)} all-gather(bf16[16,1,576]{2,0,1:T(8,128)(2,1)S(1)} %pad_maximum_fusion.4), channel_id=1, replica_groups=mesh['blk'=16,'beam'=8] {'blk'}, dimensions={1}, use_global_device_ids=true | all-gather | bytes 313344 | tf_op jit(solution)/shard_map/all_gather | solution.py:142
  39.9 3.9 copy.230
  53.5 18.3 %all_gather.91 = bf16[16,16,576]{2,0,1:T(8,128)(2,1)S(1)} all-gather(bf16[16,1,576]{2,0,1:T(8,128)(2,1)S(1)} %pad_maximum_fusion.5), channel_id=1, replica_groups=mesh['blk'=16,'beam'=8] {'blk'}, dimensions={1}, use_global_device_ids=true | all-gather | bytes 313344 | tf_op jit(solution)/shard_map/all_gather | solution.py:142
  74.8 18.9 %all_gather.98 = bf16[16,16,576]{2,0,1:T(8,128)(2,1)S(1)} all-gather(bf16[16,1,576]{2,0,1:T(8,128)(2,1)S(1)} %pad_maximum_fusion.6), channel_id=1, replica_groups=mesh['blk'=16,'beam'=8] {'blk'}, dimensions={1}, use_global_device_ids=true | all-gather | bytes 313344 | tf_op jit(solution)/shard_map/all_gather | solution.py:142
  98.2 19.3 %all_gather.105 = bf16[16,16,576]{2,0,1:T(8,128)(2,1)S(1)} all-gather(bf16[16,1,576]{2,0,1:T(8,128)(2,1)S(1)} %pad_maximum_fusion.7), channel_id=1, replica_groups=mesh['blk'=16,'beam'=8] {'blk'}, dimensions={1}, use_global_device_ids=true | all-gather | bytes 313344 | tf_op jit(solution)/shard_map/all_gather | solution.py:142
  134.6 11.5 %scatter_fusion.3 = s32[2,24]{1,0:T(2,128)S(1)} fusion(s32[2,24]{1,0:T(2,128)S(1)} %broadcast.828.clone, s32[256]{0:T(256)S(1)} %reshape.1849, s32[256]{0:T(256)S(1)} %reshape.1809), kind=kCustom, calls=%fused_computation.22 | custom fusion | bytes 5120 | tf_op jit(solution)/shard_map/scatter | solution.py:208
  167.4 11.5 %scatter_fusion.2 = s32[2,24]{1,0:T(2,128)S(1)} fusion(s32[2,24]{1,0:T(2,128)S(1)} %broadcast.828.clone.1, s32[256]{0:T(256)S(1)} %reshape.1835, s32[256]{0:T(256)S(1)} %reshape.1809), kind=kCustom, calls=%fused_computation.20 | custom fusion | bytes 5120 | tf_op jit(solution)/shard_map/scatter | solution.py:208
  184.8 11.5 %scatter_fusion.1 = s32[2,24]{1,0:T(2,128)S(1)} fusion(s32[2,24]{1,0:T(2,128)S(1)} %broadcast.828.clone.2, s32[256]{0:T(256)S(1)} %reshape.1821, s32[256]{0:T(256)S(1)} %reshape.1809), kind=kCustom, calls=%fused_computation.18 | custom fusion | bytes 5120 | tf_op jit(solution)/shard_map/scatter | solution.py:208
  200.9 18.2 %all_gather.85 = f32[16,16,16]{2,1,0:T(8,128)S(1)} all-gather(f32[1,16,16]{2,1,0:T(8,128)S(1)} %all_gather_reshape.36), channel_id=1, replica_groups=mesh['blk'=16,'beam'=8] {'blk'}, dimensions={0}, use_global_device_ids=true | all-gather | bytes 17408 | tf_op jit(solution)/shard_map/all_gather | solution.py:14
  219.1 16.3 %all_gather.86 = f32[16,16,16]{2,1,0:T(8,128)S(1)} all-gather(f32[1,16,16]{2,1,0:T(8,128)S(1)} %all_gather_reshape.37), channel_id=1, replica_groups=mesh['blk'=16,'beam'=8] {'blk'}, dimensions={0}, use_global_device_ids=true | all-gather | bytes 17408 | tf_op jit(solution)/shard_map/all_gather | solution.py:14
  235.4 20.0 %all_gather.92 = f32[16,16,16]{2,1,0:T(8,128)S(1)} all-gather(f32[1,16,16]{2,1,0:T(8,128)S(1)} %all_gather_reshape.39), channel_id=1, replica_groups=mesh['blk'=16,'beam'=8] {'blk'}, dimensions={0}, use_global_device_ids=true | all-gather | bytes 17408 | tf_op jit(solution)/shard_map/all_gather | solution.py:14
  255.4 18.1 %all_gather.93 = f32[16,16,16]{2,1,0:T(8,128)S(1)} all-gather(f32[1,16,16]{2,1,0:T(8,128)S(1)} %all_gather_reshape.40), channel_id=1, replica_groups=mesh['blk'=16,'beam'=8] {'blk'}, dimensions={0}, use_global_device_ids=true | all-gather | bytes 17408 | tf_op jit(solution)/shard_map/all_gather | solution.py:14
  273.4 18.6 %all_gather.99 = f32[16,16,16]{2,1,0:T(8,128)S(1)} all-gather(f32[1,16,16]{2,1,0:T(8,128)S(1)} %all_gather_reshape.42), channel_id=1, replica_groups=mesh['blk'=16,'beam'=8] {'blk'}, dimensions={0}, use_global_device_ids=true | all-gather | bytes 17408 | tf_op jit(solution)/shard_map/all_gather | solution.py:14
  292.0 16.2 %all_gather.100 = f32[16,16,16]{2,1,0:T(8,128)S(1)} all-gather(f32[1,16,16]{2,1,0:T(8,128)S(1)} %all_gather_reshape.43), channel_id=1, replica_groups=mesh['blk'=16,'beam'=8] {'blk'}, dimensions={0}, use_global_device_ids=true | all-gather | bytes 17408 | tf_op jit(solution)/shard_map/all_gather | solution.py:14
  308.2 20.4 %all_gather.106 = f32[16,16,16]{2,1,0:T(8,128)S(1)} all-gather(f32[1,16,16]{2,1,0:T(8,128)S(1)} %all_gather_reshape.45), channel_id=1, replica_groups=mesh['blk'=16,'beam'=8] {'blk'}, dimensions={0}, use_global_device_ids=true | all-gather | bytes 17408 | tf_op jit(solution)/shard_map/all_gather | solution.py:14
  328.6 18.1 %all_gather.107 = f32[16,16,16]{2,1,0:T(8,128)S(1)} all-gather(f32[1,16,16]{2,1,0:T(8,128)S(1)} %all_gather_reshape.46), channel_id=1, replica_groups=mesh['blk'=16,'beam'=8] {'blk'}, dimensions={0}, use_global_device_ids=true | all-gather | bytes 17408 | tf_op jit(solution)/shard_map/all_gather | solution.py:14
  355.8 39.0 %while.80 = (s32[]{:T(128)}, f32[16,16]{1,0:T(8,128)}, f32[16,16]{1,0:T(8,128)}, f32[16,16,512]{2,1,0:T(8,128)S(1)}, f32[16,16,16]{2,1,0:T(8,128)}, /*index=5*/f...) while((s32[]{:T(128)}, f32[16,16]{1,0:T(8,128)}, ...), condition=%wide.region_8.10_spmd, body=%wide.region_7.9_spmd.sunk | while | flops 394757 | bytes 1583255 | solution.py:20
  401.3 39.0 %while.81 = (s32[]{:T(128)}, f32[16,16]{1,0:T(8,128)}, f32[16,16]{1,0:T(8,128)}, f32[16,16,512]{2,1,0:T(8,128)S(1)}, f32[16,16,16]{2,1,0:T(8,128)}, /*index=5*/f...) while((s32[]{:T(128)}, f32[16,16]{1,0:T(8,128)}, ...), condition=%wide.region_23.28_spmd, body=%wide.region_22.27_spmd.sunk | while | flops 394757 | bytes 1583255 | solution.py:20
  446.9 39.0 %while.82 = (s32[]{:T(128)}, f32[16,16]{1,0:T(8,128)}, f32[16,16]{1,0:T(8,128)}, f32[16,16,512]{2,1,0:T(8,128)S(1)}, f32[16,16,16]{2,1,0:T(8,128)}, /*index=5*/f...) while((s32[]{:T(128)}, f32[16,16]{1,0:T(8,128)}, ...), condition=%wide.region_40.45_spmd, body=%wide.region_39.44_spmd.sunk | while | flops 394757 | bytes 1583255 | solution.py:20
  492.5 39.0 %while.83 = (s32[]{:T(128)}, f32[16,16]{1,0:T(8,128)}, f32[16,16]{1,0:T(8,128)}, f32[16,16,512]{2,1,0:T(8,128)S(1)}, f32[16,16,16]{2,1,0:T(8,128)}, /*index=5*/f...) while((s32[]{:T(128)}, f32[16,16]{1,0:T(8,128)}, ...), condition=%wide.region_57.62_spmd, body=%wide.region_56.61_spmd.sunk | while | flops 394757 | bytes 1583255 | solution.py:20
  538.0 3.1 fusion.97
  541.4 11.5 %scatter_fusion = s32[2,24]{1,0:T(2,128)S(1)} fusion(s32[2,24]{1,0:T(2,128)S(1)} %broadcast.828.clone.3, s32[256]{0:T(256)S(1)} %reshape.1807, s32[256]{0:T(256)S(1)} %reshape.1809), kind=kCustom, calls=%fused_computation.16 | custom fusion | bytes 5120 | tf_op jit(solution)/shard_map/scatter | solution.py:208
  565.6 22.3 %all-gather.25.cloned.1.call-done = f32[256,2048]{1,0:T(8,128)} async-done(((f32[16,2048]{1,0:T(8,128)}), f32[256,2048]{1,0:T(8,128)}) %all-gather.25.cloned.1.call-update) | async-done | bytes 2097168 | tf_op jit(solution)/shard_map/all_gather | solution.py:188
  589.6 45.0 %all-gather.27.cloned.1.call-done = f32[256,2048]{1,0:T(8,128)} async-done(((f32[16,2048]{1,0:T(8,128)}), f32[256,2048]{1,0:T(8,128)}) %all-gather.27.cloned.1.call-update) | async-done | bytes 2097168 | tf_op jit(solution)/shard_map/all_gather | solution.py:188
  639.3 16.1 %all_gather.111 = bf16[128,2048]{1,0:T(8,128)(2,1)} all-gather(bf16[16,2048]{1,0:T(8,128)(2,1)S(1)} %get-tuple-element.891), channel_id=1, replica_groups=mesh['blk'=16,'beam'=8] {'beam'}, dimensions={0}, use_global_device_ids=true | all-gather | bytes 589824 | tf_op jit(solution)/shard_map/all_gather | solution.py:191
  657.4 14.3 %all_gather.104 = bf16[128,2048]{1,0:T(8,128)(2,1)} all-gather(bf16[16,2048]{1,0:T(8,128)(2,1)S(1)} %get-tuple-element.890), channel_id=1, replica_groups=mesh['blk'=16,'beam'=8] {'beam'}, dimensions={0}, use_global_device_ids=true | all-gather | bytes 589824 | tf_op jit(solution)/shard_map/all_gather | solution.py:191
  672.7 14.2 %all_gather.97 = bf16[128,2048]{1,0:T(8,128)(2,1)} all-gather(bf16[16,2048]{1,0:T(8,128)(2,1)S(1)} %get-tuple-element.889), channel_id=1, replica_groups=mesh['blk'=16,'beam'=8] {'beam'}, dimensions={0}, use_global_device_ids=true | all-gather | bytes 589824 | tf_op jit(solution)/shard_map/all_gather | solution.py:191
  687.7 14.3 %all_gather.90 = bf16[128,2048]{1,0:T(8,128)(2,1)} all-gather(bf16[16,2048]{1,0:T(8,128)(2,1)S(1)} %get-tuple-element.888), channel_id=1, replica_groups=mesh['blk'=16,'beam'=8] {'beam'}, dimensions={0}, use_global_device_ids=true | all-gather | bytes 589824 | tf_op jit(solution)/shard_map/all_gather | solution.py:191
  703.0 2.8 gather_fusion.14
  705.8 3.5 fusion.67
  709.3 4.0 convolution_multiply_fusion
  713.3 2.6 scatter_custom_fusion.7
  715.9 2.7 gather_fusion.10
  718.6 3.5 fusion.66
  722.0 3.9 convolution_multiply_fusion.1
  725.9 2.7 scatter_custom_fusion.5
  728.6 2.7 fusion.13
  731.4 2.7 fusion.15
  734.1 2.7 gather_fusion.6
  736.7 2.8 fusion.65
  739.6 4.0 convolution_multiply_fusion.2
  743.6 2.8 scatter_custom_fusion.3
  746.5 2.7 fusion.17
  751.3 3.4 fusion.64
  754.7 3.9 convolution_multiply_fusion.3
  758.6 2.6 scatter_custom_fusion.1
  761.2 2.7 fusion.19
  764.0 153.4 %all-reduce.11.cloned.1.call-done = (f32[128,2048]{1,0:T(8,128)}, f32[128,2048]{1,0:T(8,128)}, f32[128,2048]{1,0:T(8,128)}, f32[128,2048]{1,0:T(8,128)}) async-done(((f32[128,2048]{1,0:T(8,128)}, f32[128,2048]{1,0:T(8,128)}, f32[128,2048]{1,0:T(8,128)}, f32[128,2048]{1,0:T(8,128)}), (f32[128,2048]{1,0:T(8,128)}, f32[128,2048]{1,0:T(8,128)}, f32[128,2048]{1,0:T(8,128)}, ...) | async-done | bytes 4194320
  (563 shorter events, 297.3 us)
Async XLA Ops:
  6.5 702.7 %copy-start = (bf16[2,352,2048]{2,1,0:T(8,128)(2,1)S(1)}, bf16[2,352,2048]{2,1,0:T(8,128)(2,1)}, u32[]{:S(2)}) copy-start(bf16[2,352,2048]{2,1,0:T(8,128)(2,1)} %param.59) | copy-start | bytes 8650756
  6.5 348.1 %all-gather.13.cloned.1.call-start = ((), (), s32[]{:S(2)}) async-start(), calls=%async_computation | async-start | bytes 8912896 | tf_op jit(solution)/shard_map/all_gather | solution.py:14
  48.0 352.3 %all-gather.15.cloned.1.call-start = ((), (), s32[]{:S(2)}) async-start(), calls=%async_computation.1 | async-start | bytes 8912896 | tf_op jit(solution)/shard_map/all_gather | solution.py:14
  48.5 23.6 %copy-start.2 = (bf16[2,6,128,576]{3,2,1,0:T(8,128)(2,1)S(1)}, bf16[2,6,128,576]{3,2,1,0:T(8,128)(2,1)}, u32[]{:S(2)}) copy-start(bf16[2,6,128,576]{3,2,1,0:T(8,128)(2,1)} %copy.230) | copy-start | bytes 5308420
  74.5 371.3 %all-gather.17.cloned.1.call-start = ((), (), s32[]{:S(2)}) async-start(), calls=%async_computation.2 | async-start | bytes 8912896 | tf_op jit(solution)/shard_map/all_gather | solution.py:14
  74.7 22.0 %copy-start.3 = (bf16[2,6,128,576]{3,2,1,0:T(8,128)(2,1)S(1)}, bf16[2,6,128,576]{3,2,1,0:T(8,128)(2,1)}, u32[]{:S(2)}) copy-start(bf16[2,6,128,576]{3,2,1,0:T(8,128)(2,1)} %copy.230) | copy-start | bytes 5308420
  97.9 393.5 %all-gather.19.cloned.1.call-start = ((), (), s32[]{:S(2)}) async-start(), calls=%async_computation.3 | async-start | bytes 8912896 | tf_op jit(solution)/shard_map/all_gather | solution.py:14
  98.1 22.3 %copy-start.4 = (bf16[2,6,128,576]{3,2,1,0:T(8,128)(2,1)S(1)}, bf16[2,6,128,576]{3,2,1,0:T(8,128)(2,1)}, u32[]{:S(2)}) copy-start(bf16[2,6,128,576]{3,2,1,0:T(8,128)(2,1)} %copy.230) | copy-start | bytes 5308420
  121.6 440.4 %all-gather.21.cloned.1.call-start = ((), (), s32[]{:S(2)}) async-start(), calls=%async_computation.4 | async-start | bytes 2228224 | tf_op jit(solution)/shard_map/all_gather | solution.py:188
  134.5 12.1 %copy-start.51 = (s32[2,8,1]{1,0,2:T(2,128)S(1)}, s32[2,8,1]{1,0,2:T(2,128)}, u32[]{:S(2)}) copy-start(s32[2,8,1]{1,0,2:T(2,128)} %get-tuple-element.930) | copy-start | bytes 196
  134.5 12.2 %copy-start.53 = (f32[16]{0:T(128)S(1)}, f32[16]{0:T(128)}, u32[]{:S(2)}) copy-start(f32[16]{0:T(128)} %multiply_reduce_fusion.4) | copy-start | bytes 196
  134.5 12.2 %copy-start.52 = (f32[16]{0:T(128)S(1)}, f32[16]{0:T(128)}, u32[]{:S(2)}) copy-start(f32[16]{0:T(128)} %multiply_reduce_fusion.6) | copy-start | bytes 196
  134.5 12.2 %copy-start.37 = (f32[512]{0:T(512)S(1)}, f32[512]{0:T(512)}, u32[]{:S(2)}) copy-start(f32[512]{0:T(512)} %param.49) | copy-start | bytes 6148
  134.5 12.3 %copy-start.50 = (s32[2,8,1]{1,0,2:T(2,128)S(1)}, s32[2,8,1]{1,0,2:T(2,128)}, u32[]{:S(2)}) copy-start(s32[2,8,1]{1,0,2:T(2,128)} %get-tuple-element.931) | copy-start | bytes 196
  134.5 13.2 %copy-start.40 = (pred[2,8]{1,0:T(4,128)(4,1)S(1)}, pred[2,8]{1,0:T(4,128)(4,1)}, u32[]{:S(2)}) copy-start(pred[2,8]{1,0:T(4,128)(4,1)} %get-tuple-element.928) | copy-start | bytes 52
  167.4 14.5 %copy-start.39 = (pred[128,2]{0,1:T(4,128)(4,1)S(1)}, pred[128,2]{0,1:T(4,128)(4,1)}, u32[]{:S(2)}) copy-start(pred[128,2]{0,1:T(4,128)(4,1)} %get-tuple-element.798) | copy-start | bytes 772
  184.8 14.5 %copy-start.38 = (pred[128,2]{0,1:T(4,128)(4,1)S(1)}, pred[128,2]{0,1:T(4,128)(4,1)}, u32[]{:S(2)}) copy-start(pred[128,2]{0,1:T(4,128)(4,1)} %get-tuple-element.797) | copy-start | bytes 772
  219.1 134.8 %copy-start.24 = (f32[16,16,16]{2,1,0:T(8,128)}, f32[16,16,16]{2,1,0:T(8,128)S(1)}, u32[]{:S(2)}) copy-start(f32[16,16,16]{2,1,0:T(8,128)S(1)} %all_gather.85) | copy-start | bytes 49156
  235.4 118.5 %copy-start.25 = (f32[16,16,16]{2,1,0:T(8,128)}, f32[16,16,16]{2,1,0:T(8,128)S(1)}, u32[]{:S(2)}) copy-start(f32[16,16,16]{2,1,0:T(8,128)S(1)} %all_gather.86) | copy-start | bytes 49156
  255.4 98.5 %copy-start.22 = (f32[16,16,16]{2,1,0:T(8,128)}, f32[16,16,16]{2,1,0:T(8,128)S(1)}, u32[]{:S(2)}) copy-start(f32[16,16,16]{2,1,0:T(8,128)S(1)} %all_gather.92) | copy-start | bytes 49156
  273.4 80.4 %copy-start.23 = (f32[16,16,16]{2,1,0:T(8,128)}, f32[16,16,16]{2,1,0:T(8,128)S(1)}, u32[]{:S(2)}) copy-start(f32[16,16,16]{2,1,0:T(8,128)S(1)} %all_gather.93) | copy-start | bytes 49156
  292.0 61.8 %copy-start.20 = (f32[16,16,16]{2,1,0:T(8,128)}, f32[16,16,16]{2,1,0:T(8,128)S(1)}, u32[]{:S(2)}) copy-start(f32[16,16,16]{2,1,0:T(8,128)S(1)} %all_gather.99) | copy-start | bytes 49156
  308.2 45.6 %copy-start.21 = (f32[16,16,16]{2,1,0:T(8,128)}, f32[16,16,16]{2,1,0:T(8,128)S(1)}, u32[]{:S(2)}) copy-start(f32[16,16,16]{2,1,0:T(8,128)S(1)} %all_gather.100) | copy-start | bytes 49156
  328.6 25.2 %copy-start.18 = (f32[16,16,16]{2,1,0:T(8,128)}, f32[16,16,16]{2,1,0:T(8,128)S(1)}, u32[]{:S(2)}) copy-start(f32[16,16,16]{2,1,0:T(8,128)S(1)} %all_gather.106) | copy-start | bytes 49156
  355.7 42.3 %copy-start.10 = (bf16[1,512,128]{2,1,0:T(8,128)(2,1)S(1)}, bf16[1,512,128]{2,1,0:T(8,128)(2,1)}, u32[]{:S(2)}) copy-start(bf16[1,512,128]{2,1,0:T(8,128)(2,1)} %param.51) | copy-start | bytes 393220
  400.2 163.6 %all-gather.23.cloned.1.call-start = ((), (), s32[]{:S(2)}) async-start(), calls=%async_computation.5 | async-start | bytes 2228224 | tf_op jit(solution)/shard_map/all_gather | solution.py:188
  445.7 142.2 %all-gather.25.cloned.1.call-start = ((), (), s32[]{:S(2)}) async-start(), calls=%async_computation.6 | async-start | bytes 2228224 | tf_op jit(solution)/shard_map/all_gather | solution.py:188
  491.4 143.3 %all-gather.27.cloned.1.call-start = ((), (), s32[]{:S(2)}) async-start(), calls=%async_computation.7 | async-start | bytes 2228224 | tf_op jit(solution)/shard_map/all_gather | solution.py:188
  536.9 380.4 %all-reduce.11.cloned.1.call-start = ((), (), s32[]{:S(2)}) async-start(), calls=%async_computation.8 | async-start | bytes 8388608
  541.3 11.6 %copy-start.32 = (f32[128,2]{0,1:T(2,128)S(1)}, f32[128,2]{0,1:T(2,128)}, u32[]{:S(2)}) copy-start(f32[128,2]{0,1:T(2,128)} %get-tuple-element.793) | copy-start | bytes 3076
  541.3 13.0 %copy-start.54 = (s32[48]{0:T(128)S(1)}, s32[48]{0:T(128)}, u32[]{:S(2)}) copy-start(s32[48]{0:T(128)} %reshape.1978) | copy-start | bytes 580
  541.3 13.6 %copy-start.55 = (s32[48]{0:T(128)S(1)}, s32[48]{0:T(128)}, u32[]{:S(2)}) copy-start(s32[48]{0:T(128)} %reshape.1960) | copy-start | bytes 580
  541.3 13.6 %copy-start.56 = (s32[48]{0:T(128)S(1)}, s32[48]{0:T(128)}, u32[]{:S(2)}) copy-start(s32[48]{0:T(128)} %reshape.1942) | copy-start | bytes 580
  541.3 14.2 %copy-start.58 = (s32[48,1]{0,1:T(1,128)S(1)}, s32[48,1]{0,1:T(1,128)}, u32[]{:S(2)}) copy-start(s32[48,1]{0,1:T(1,128)} %reshape.1683) | copy-start | bytes 580
  541.3 14.7 %copy-start.59 = (s32[48,1]{0,1:T(1,128)S(1)}, s32[48,1]{0,1:T(1,128)}, u32[]{:S(2)}) copy-start(s32[48,1]{0,1:T(1,128)} %reshape.1674) | copy-start | bytes 580
  541.3 15.2 %copy-start.60 = (s32[48,1]{0,1:T(1,128)S(1)}, s32[48,1]{0,1:T(1,128)}, u32[]{:S(2)}) copy-start(s32[48,1]{0,1:T(1,128)} %reshape.1665) | copy-start | bytes 580
  541.3 18.4 %copy-start.47 = (f32[2,24]{1,0:T(2,128)S(1)}, f32[2,24]{1,0:T(2,128)}, u32[]{:S(2)}) copy-start(f32[2,24]{1,0:T(2,128)} %reshape.1986) | copy-start | bytes 580
  541.3 19.0 %copy-start.48 = (f32[2,24]{1,0:T(2,128)S(1)}, f32[2,24]{1,0:T(2,128)}, u32[]{:S(2)}) copy-start(f32[2,24]{1,0:T(2,128)} %reshape.1968) | copy-start | bytes 580
  541.3 19.6 %copy-start.49 = (f32[2,24]{1,0:T(2,128)S(1)}, f32[2,24]{1,0:T(2,128)}, u32[]{:S(2)}) copy-start(f32[2,24]{1,0:T(2,128)} %reshape.1950) | copy-start | bytes 580
  563.8 73.2 %copy-start.8 = (bf16[4,16,2048]{2,1,0:T(8,128)(2,1)S(1)}, bf16[4,16,2048]{2,1,0:T(8,128)(2,1)}, u32[]{:S(2)}) copy-start(bf16[4,16,2048]{2,1,0:T(8,128)(2,1)} %param.45) | copy-start | bytes 786436
  565.5 72.7 %copy-start.29 = (f32[2048]{0:T(1024)S(1)}, f32[2048]{0:T(1024)}, u32[]{:S(2)}) copy-start(f32[2048]{0:T(1024)} %param.53) | copy-start | bytes 24580
  637.0 34.8 %copy-start.6 = (bf16[2048,176]{0,1:T(8,128)(2,1)S(1)}, bf16[2048,176]{0,1:T(8,128)(2,1)}, u32[]{:S(2)}) copy-start(bf16[2048,176]{0,1:T(8,128)(2,1)} %param.54) | copy-start | bytes 2162692
  639.3 47.5 %copy-start.13 = (bf16[16,2048]{1,0:T(8,128)(2,1)}, bf16[16,2048]{1,0:T(8,128)(2,1)S(1)}, u32[]{:S(2)}) copy-start(bf16[16,2048]{1,0:T(8,128)(2,1)S(1)} %get-tuple-element.889) | copy-start | bytes 196612
  639.3 48.4 %copy-start.15 = (bf16[16,2048]{1,0:T(8,128)(2,1)}, bf16[16,2048]{1,0:T(8,128)(2,1)S(1)}, u32[]{:S(2)}) copy-start(bf16[16,2048]{1,0:T(8,128)(2,1)S(1)} %get-tuple-element.890) | copy-start | bytes 196612
  639.3 48.4 %copy-start.16 = (bf16[16,2048]{1,0:T(8,128)(2,1)}, bf16[16,2048]{1,0:T(8,128)(2,1)S(1)}, u32[]{:S(2)}) copy-start(bf16[16,2048]{1,0:T(8,128)(2,1)S(1)} %get-tuple-element.891) | copy-start | bytes 196612
  639.3 62.8 %copy-start.11 = (bf16[16,2048]{1,0:T(8,128)(2,1)}, bf16[16,2048]{1,0:T(8,128)(2,1)S(1)}, u32[]{:S(2)}) copy-start(bf16[16,2048]{1,0:T(8,128)(2,1)S(1)} %get-tuple-element.888) | copy-start | bytes 196612
  657.4 48.3 %copy-start.46 = (pred[2,24]{1,0:T(4,128)(4,1)S(1)}, pred[2,24]{1,0:T(4,128)(4,1)}, u32[]{:S(2)}) copy-start(pred[2,24]{1,0:T(4,128)(4,1)} %compare_and_fusion) | copy-start | bytes 148
  709.3 9.3 %copy-start.45 = (pred[2,24]{1,0:T(4,128)(4,1)S(1)}, pred[2,24]{1,0:T(4,128)(4,1)}, u32[]{:S(2)}) copy-start(pred[2,24]{1,0:T(4,128)(4,1)} %compare_and_fusion.1) | copy-start | bytes 148
  (22 other events, 108.6 us)
Sparse Core Ops, SparseCore 0:
  48.1 78.7 all-gather.12
  129.0 70.3 all-gather.14
  201.6 71.7 all-gather.16
  275.4 71.6 all-gather.18
  400.3 94.1 all-gather.20
  496.5 44.5 all-gather.22
  543.3 44.5 all-gather.24
  590.0 44.5 all-gather.26
  764.1 153.2 all-reduce.10
